TPU v7x, 256 devices: a whole 4x4x8 slice. The times are simulated.
256 devices in a mesh: section: 32 (over x_lo, z, core), expert: 8 (over x_hi, y).
Axes of the slice: x: 4 (x_hi: 2, x_lo: 2; x = x_hi * 2 + x_lo), y: 4, z: 8, core: 2. Of those that a mesh axis runs over, the one named last changes fastest.
Arguments:
- tokens: bfloat16 [2048, 3072], P(('section', 'expert')), may hold values from -6 to 6
- upstream: bfloat16 [2048, 3072], P(('section', 'expert')), may hold values from -2 to 2
- route_ids: int32 [2048, 2], P(('section', 'expert')), may hold values from 0 to 7, all different within a row; in each aligned block of 8 rows (0 to 7, 8 to 15, ...) at most 4 rows name the same one
- route_gates: bfloat16 [2048, 2], P(('section', 'expert')), may hold values from 0.099609375 to 0.8984375
- w_gate: bfloat16 [8, 3072, 8192], P('expert', None, 'section'), may hold values from -0.109375 to 0.109375
- w_up: bfloat16 [8, 3072, 8192], P('expert', None, 'section'), may hold values from -0.109375 to 0.109375
- w_down: bfloat16 [8, 8192, 3072], P('expert', 'section'), may hold values from -0.0625 to 0.0625
Outputs:
- grad_tokens: bfloat16 [2048, 3072], P(('section', 'expert'))
- grad_gates: float32 [2048, 2], P(('section', 'expert'))
- grad_w_gate: bfloat16 [8, 3072, 8192], P('expert', None, 'section')
- grad_w_up: bfloat16 [8, 3072, 8192], P('expert', None, 'section')
- grad_w_down: bfloat16 [8, 8192, 3072], P('expert', 'section')
Inputs may be any that keep to these rules, and one draw needn't show every extreme that they name: `route_ids`: the two experts of a token differ. Among the 16 choices of the tokens of one device, each expert is named at most 4 times, and in some device's tokens some expert is named exactly 4 times.
All inputs are finite; a program needn't handle non-finite values.
Results may differ from a plain program's by a relative error of at most 0.0058.
Values may be sent and summed in bfloat16 or wider, within the bound.
A program may use at most 128 MiB of HBM per device.

v0:
```python
import jax
import jax.numpy as jnp
from jax import lax
from jax.sharding import PartitionSpec as P


def slot_matrix(route_ids, experts, capacity):
    flattened = route_ids.reshape(-1)
    onehot = (flattened[:, None] == jnp.arange(experts, dtype=jnp.int32)[None, :]).astype(jnp.int32)
    before = jnp.cumsum(onehot, axis=0) - onehot
    position = jnp.sum(before * onehot, axis=1)
    target = flattened * capacity + position
    columns = jnp.arange(experts * capacity, dtype=jnp.int32)
    return target[:, None] == columns[None, :]


def contract_last(left, right):
    return lax.dot_general(
        left, right, (((1,), (1,)), ((), ())), preferred_element_type=jnp.float32
    )


def contract_first(left, right):
    return lax.dot_general(
        left, right, (((0,), (0,)), ((), ())), preferred_element_type=jnp.float32
    )


def local(tokens, upstream, route_ids, route_gates, w_gate, w_up, w_down):
    experts = lax.axis_size("expert")
    tok_count, features = tokens.shape
    capacity = min(tok_count, max(2, 4 * tok_count // experts))
    chosen_slots = slot_matrix(route_ids, experts, capacity)
    placement = chosen_slots.astype(jnp.bfloat16)
    tokens_twice = jnp.repeat(tokens, 2, axis=0)
    upstream_twice = jnp.repeat(upstream, 2, axis=0)
    send_x = (
        contract_first(placement, tokens_twice)
        .astype(jnp.bfloat16)
        .reshape(experts, capacity, features)
    )
    send_dy = (
        contract_first(placement, upstream_twice)
        .astype(jnp.bfloat16)
        .reshape(experts, capacity, features)
    )
    send_weight = (
        jnp.dot(
            route_gates.reshape(-1).astype(jnp.float32),
            chosen_slots.astype(jnp.float32),
            precision=lax.Precision.HIGHEST,
        )
        .astype(jnp.bfloat16)
        .reshape(experts, capacity)
    )
    recv_x, recv_dy, recv_weight = (
        lax.all_to_all(send_x, "expert", split_axis=0, concat_axis=0, tiled=True),
        lax.all_to_all(send_dy, "expert", split_axis=0, concat_axis=0, tiled=True),
        lax.all_to_all(send_weight, "expert", split_axis=0, concat_axis=0, tiled=True),
    )
    every_x, every_dy, every_weight = (
        lax.all_gather(recv_x, "section", axis=0, tiled=True),
        lax.all_gather(recv_dy, "section", axis=0, tiled=True),
        lax.all_gather(recv_weight, "section", axis=0, tiled=True),
    )
    row_count = every_x.shape[0] * capacity
    rows_x = every_x.reshape(row_count, features)
    rows_dy = every_dy.reshape(row_count, features)
    weight = every_weight.reshape(row_count, 1).astype(jnp.float32)
    gate_slab = w_gate[0]
    up_slab = w_up[0]
    down_slab = w_down[0]
    pre_gate = jnp.dot(rows_x, gate_slab, preferred_element_type=jnp.float32)
    pre_up = jnp.dot(rows_x, up_slab, preferred_element_type=jnp.float32)
    sigmoid_gate = jax.nn.sigmoid(pre_gate)
    active = pre_gate * sigmoid_gate
    hidden = (active * pre_up).astype(jnp.bfloat16)
    back_proj = contract_last(rows_dy, down_slab)
    d_hidden = weight * back_proj
    d_gate = (d_hidden * pre_up * (sigmoid_gate * (1.0 + pre_gate * (1.0 - sigmoid_gate)))).astype(
        jnp.bfloat16
    )
    d_up = (d_hidden * active).astype(jnp.bfloat16)
    scaled_up = (weight * rows_dy.astype(jnp.float32)).astype(jnp.bfloat16)
    grad_down = contract_first(hidden, scaled_up)
    grad_gate = contract_first(rows_x, d_gate)
    grad_up = contract_first(rows_x, d_up)
    input_part = contract_last(d_gate, gate_slab) + contract_last(d_up, up_slab)
    own_rows = experts * capacity
    output_part = jnp.dot(hidden, down_slab, preferred_element_type=jnp.float32)
    input_mine, output_mine = (
        lax.psum_scatter(input_part, "section", scatter_dimension=0, tiled=True),
        lax.psum_scatter(output_part, "section", scatter_dimension=0, tiled=True),
    )
    gate_mine = jnp.sum(
        recv_dy.reshape(own_rows, features).astype(jnp.float32) * output_mine, axis=1
    )
    back_input, back_gate = (
        lax.all_to_all(
            input_mine.reshape(experts, capacity, features),
            "expert",
            split_axis=0,
            concat_axis=0,
            tiled=True,
        ),
        lax.all_to_all(
            gate_mine.reshape(experts, capacity), "expert", split_axis=0, concat_axis=0, tiled=True
        ),
    )
    selector = chosen_slots.astype(jnp.float32)
    choice_grads = jnp.dot(
        selector, back_input.reshape(own_rows, features), precision=lax.Precision.HIGHEST
    )
    grad_tokens = jnp.sum(choice_grads.reshape(tok_count, 2, features), axis=1).astype(jnp.bfloat16)
    grad_gates = jnp.dot(
        selector, back_gate.reshape(own_rows), precision=lax.Precision.HIGHEST
    ).reshape(tok_count, 2)
    return (
        grad_tokens,
        grad_gates,
        grad_gate.astype(jnp.bfloat16)[None],
        grad_up.astype(jnp.bfloat16)[None],
        grad_down.astype(jnp.bfloat16)[None],
    )


def solution(mesh):
    placed = (
        P(("section", "expert"), None),
        P(("section", "expert"), None),
        P(("section", "expert"), None),
        P(("section", "expert"), None),
        P("expert", None, "section"),
        P("expert", None, "section"),
        P("expert", "section", None),
    )
    return jax.shard_map(
        local,
        mesh=mesh,
        in_specs=placed,
        out_specs=(
            P(("section", "expert"), None),
            P(("section", "expert"), None),
            P("expert", None, "section"),
            P("expert", None, "section"),
            P("expert", "section", None),
        ),
        check_vma=False,
    )
```

profile of v0, /device:TPU:4, one launch (start us, length us, event | category | flops | bytes accessed | tf_op | source)
XLA Modules:
  0.0 489.4 jit_solution(14757666695438629461)
XLA Ops:
  7.2 0.0 copy-start
  7.2 0.0 all-gather.6.cloned.1.call-start
  7.2 0.9 copy.26
  8.1 0.1 eq.55
  8.2 0.1 fusion.22
  8.3 0.2 select_reduce_fusion
  8.5 0.9 broadcast_in_dim.19
  9.4 0.3 convolution_convert_fusion.2
  9.7 0.1 reshape.117
  9.8 12.8 %all_to_all.37 = bf16[8,4,3072]{2,1,0:T(4,128)(2,1)} all-to-all(bf16[8,4,3072]{2,1,0:T(4,128)(2,1)S(1)} %reshape.117), channel_id=1, replica_groups=mesh['section'=32,'expert'=8] {'expert'}, dimensions={0} | all-to-all | bytes 393216 | tf_op jit(solution)/shard_map/all_to_all | solution.py:57
  22.6 0.0 all-gather.6.cloned.1.call-update
  22.7 0.0 all-gather.4.cloned.1.call-start
  22.7 0.9 broadcast_in_dim.18
  23.6 0.3 convolution_convert_fusion.3
  23.9 0.1 reshape.114
  24.0 11.5 %all_to_all.38 = bf16[8,4,3072]{2,1,0:T(4,128)(2,1)} all-to-all(bf16[8,4,3072]{2,1,0:T(4,128)(2,1)S(1)} %reshape.114), channel_id=1, replica_groups=mesh['section'=32,'expert'=8] {'expert'}, dimensions={0} | all-to-all | bytes 393216 | tf_op jit(solution)/shard_map/all_to_all | solution.py:58
  35.5 0.0 all-gather.4.cloned.1.call-update
  35.6 0.0 reduce-scatter.5.cloned.1.call-start
  35.6 0.7 copy.29
  36.4 0.1 reshape.127
  36.4 0.2 fusion.20
  36.6 0.1 all_to_all.31
  36.7 10.2 %all_to_all.39 = bf16[8,1,4]{2,1,0:T(2,128)(2,1)S(1)} all-to-all(bf16[8,1,4]{2,1,0:T(2,128)(2,1)S(1)} %all_to_all.31), channel_id=1, replica_groups=mesh['section'=32,'expert'=8] {'expert'}, dimensions={0} | all-to-all | bytes 128 | tf_op jit(solution)/shard_map/all_to_all | solution.py:59
  46.9 37.2 %all-gather = bf16[256,1,4]{2,1,0:T(2,128)(2,1)S(1)} all-gather(bf16[8,1,4]{2,1,0:T(2,128)(2,1)S(1)} %all_to_all.39), channel_id=2, replica_groups=mesh['section'=32,'expert'=8] {'section'}, dimensions={0}, use_global_device_ids=true | all-gather | bytes 2112 | tf_op jit(solution)/shard_map/all_gather | solution.py:64
  84.1 0.4 convert_reduce_fusion
  84.5 0.1 reshape.122
  84.6 0.0 copy-start.5
  84.6 8.8 %all-gather.6.cloned.1.call-done = bf16[256,4,3072]{2,1,0:T(4,128)(2,1)} async-done(((bf16[8,4,3072]{2,1,0:T(4,128)(2,1)}), bf16[256,4,3072]{2,1,0:T(4,128)(2,1)}) %all-gather.6.cloned.1.call-update) | async-done | bytes 6291472 | tf_op jit(solution)/shard_map/all_gather | solution.py:62
  93.5 10.6 %reshape.118 = bf16[1024,3072]{1,0:T(8,128)(2,1)} reshape(bf16[256,4,3072]{2,1,0:T(4,128)(2,1)} %all-gather.6.cloned.1.call-done) | data formatting | bytes 12582912 | tf_op jit(solution)/shard_map/reshape | solution.py:67
  104.1 0.0 copy-done.5
  104.1 5.6 %fusion.8 = f32[1024,256]{1,0:T(8,128)} fusion(bf16[1024,3072]{1,0:T(8,128)(2,1)} %reshape.118, bf16[1,3072,256]{2,1,0:T(8,128)(2,1)S(1)} %copy-done.5), kind=kOutput, calls=%fused_computation.14 | convolution fusion | flops 1610612736 | bytes 8912896 | tf_op jit(solution)/shard_map/dot_general | solution.py:73
  109.7 54.0 %all-gather.4.cloned.1.call-done = bf16[256,4,3072]{2,1,0:T(4,128)(2,1)} async-done(((bf16[8,4,3072]{2,1,0:T(4,128)(2,1)}), bf16[256,4,3072]{2,1,0:T(4,128)(2,1)}) %all-gather.4.cloned.1.call-update) | async-done | bytes 6291472 | tf_op jit(solution)/shard_map/all_gather | solution.py:63
  163.7 10.7 %reshape.115 = bf16[1024,3072]{1,0:T(8,128)(2,1)} reshape(bf16[256,4,3072]{2,1,0:T(4,128)(2,1)} %all-gather.4.cloned.1.call-done) | data formatting | bytes 12582912 | tf_op jit(solution)/shard_map/reshape | solution.py:68
  174.4 0.0 copy-done.3
  174.4 4.7 fusion.17
  179.1 0.0 copy-start.4
  179.1 5.0 %multiply_convert_fusion.6 = (bf16[1024,256]{1,0:T(8,128)(2,1)S(1)}, bf16[1024,256]{1,0:T(8,128)(2,1)S(1)}, bf16[1024,256]{1,0:T(8,128)(2,1)S(1)}) fusion(f32[1024,256]{1,0:T(8,128)S(1)} %copy-done.6, f32[1024,256]{1,0:T(8,128)S(1)} %fusion.17, bf16[1024,3072]{1,0:T(8,128)(2,1)} %reshape.118, bf16[1,3072,256]{2,1,0:T(8,128)(2,1)S(1)} %copy-done), kind=kOutput, calls=%fused_computation.27 | convolution fusion | flops 1614544896 | bytes 11534336 | tf_op jit(solution)/shard_map/dot_general | solution.py:74
  184.2 6.3 %fusion.13 = f32[1024,3072]{1,0:T(8,128)} fusion(bf16[1024,256]{1,0:T(8,128)(2,1)S(1)} %get-tuple-element.5, bf16[1,256,3072]{2,1,0:T(8,128)(2,1)S(1)} %copy-done.4), kind=kOutput, calls=%fused_computation.19 | convolution fusion | flops 1610612736 | bytes 14680064 | tf_op jit(solution)/shard_map/dot_general | solution.py:90
  190.5 0.0 reduce-scatter.5.cloned.1.call-update
  190.5 0.2 reduce-scatter.3.cloned.1.call-start
  190.7 3.2 fusion.6
  194.0 6.4 %convolution_add_fusion = f32[1024,3072]{1,0:T(8,128)} fusion(f32[1024,3072]{1,0:T(8,128)S(1)} %fusion.6, bf16[1024,256]{1,0:T(8,128)(2,1)S(1)} %get-tuple-element.7, bf16[1,3072,256]{2,1,0:T(8,128)(2,1)S(1)} %copy-done), kind=kOutput, calls=%fused_computation.1 | convolution fusion | flops 1613758464 | bytes 27262976 | tf_op jit(solution)/shard_map/dot_general | solution.py:18
  200.4 0.0 reduce-scatter.3.cloned.1.call-update
  200.4 0.1 reduce_sum.30
  200.5 0.1 copy.28
  200.6 0.7 copy-done.2
  201.3 6.0 %fusion.4 = bf16[1,3072,256]{2,1,0:T(8,128)(2,1)} fusion(bf16[1024,3072]{1,0:T(8,128)(2,1)} %reshape.118, bf16[1024,256]{1,0:T(8,128)(2,1)S(1)} %get-tuple-element.6), kind=kOutput, calls=%fused_computation.8 | convolution fusion | flops 1611399168 | bytes 8388608 | tf_op jit(solution)/shard_map/dot_general | solution.py:24
  207.4 6.0 %fusion.5 = bf16[1,3072,256]{2,1,0:T(8,128)(2,1)} fusion(bf16[1024,3072]{1,0:T(8,128)(2,1)} %reshape.118, bf16[1024,256]{1,0:T(8,128)(2,1)S(1)} %get-tuple-element.7), kind=kOutput, calls=%fused_computation.9 | convolution fusion | flops 1611399168 | bytes 8388608 | tf_op jit(solution)/shard_map/dot_general | solution.py:24
  213.3 114.6 %reduce-scatter.5.cloned.1.call-done = f32[32,3072]{1,0:T(8,128)} async-done(((f32[1024,3072]{1,0:T(8,128)}), f32[32,3072]{1,0:T(8,128)}) %reduce-scatter.5.cloned.1.call-update) | async-done | bytes 393232 | tf_op jit(solution)/shard_map/reduce_scatter | solution.py:93
  327.9 1.1 multiply_reduce_fusion
  329.0 0.7 all_to_all.29
  329.7 7.7 %all-to-all-start.4 = ((f32[8,1,4]{2,1,0:T(1,128)}), f32[8,1,4]{2,1,0:T(1,128)S(1)}, u32[]{:S(2)}, u32[]{:S(2)}) async-start(f32[8,1,4]{2,1,0:T(1,128)} %bitcast.5), calls=%async_computation.6 | async-start | bytes 8192 | tf_op jit(solution)/shard_map/all_to_all | solution.py:106
  337.4 126.7 %reduce-scatter.3.cloned.1.call-done = f32[32,3072]{1,0:T(8,128)} async-done(((f32[1024,3072]{1,0:T(8,128)}), f32[32,3072]{1,0:T(8,128)}) %reduce-scatter.3.cloned.1.call-update) | async-done | bytes 393232 | tf_op jit(solution)/shard_map/reduce_scatter | solution.py:92
  464.1 1.9 reshape.119
  465.9 0.0 all-to-all-done.4
  465.9 7.6 %all-to-all-start.3 = ((f32[8,4,3072]{2,1,0:T(4,128)}), f32[8,4,3072]{2,1,0:T(4,128)S(1)}, u32[]{:S(2)}, u32[]{:S(2)}) async-start(f32[8,4,3072]{2,1,0:T(4,128)} %reshape.119), calls=%async_computation.4 | async-start | bytes 786432 | tf_op jit(solution)/shard_map/all_to_all | solution.py:99
  473.6 6.1 %fusion.3 = bf16[1,256,3072]{2,1,0:T(8,128)(2,1)} fusion(bf16[1024,256]{1,0:T(8,128)(2,1)S(1)} %get-tuple-element.5, bf16[1024,3072]{1,0:T(8,128)(2,1)} %reshape.115, f32[1024]{0:T(1024)S(1)} %reshape.122), kind=kOutput, calls=%fused_computation.7 | convolution fusion | flops 1620836352 | bytes 8392704 | tf_op jit(solution)/shard_map/dot_general | solution.py:24
  479.7 0.5 broadcast.64
  480.2 0.7 reduce.7
  480.8 0.1 reshape.130
  480.9 0.8 fusion.24
  481.8 0.0 all-to-all-done.3
  481.8 0.1 reshape.129
  481.9 0.9 convolution_reduce_fusion
  (14 shorter events, 0.2 us)
Async XLA Ops:
  7.2 171.9 %copy-start = (bf16[1,3072,256]{2,1,0:T(8,128)(2,1)S(1)}, bf16[1,3072,256]{2,1,0:T(8,128)(2,1)}, u32[]{:S(2)}) copy-start(bf16[1,3072,256]{2,1,0:T(8,128)(2,1)} %param.12) | copy-start | bytes 4718596
  7.2 86.3 %all-gather.6.cloned.1.call-start = ((), (), s32[]{:S(2)}) async-start(), calls=%async_computation.8 | async-start | bytes 6488064 | tf_op jit(solution)/shard_map/all_gather | solution.py:62
  22.7 141.0 %all-gather.4.cloned.1.call-start = ((), (), s32[]{:S(2)}) async-start(), calls=%async_computation.7 | async-start | bytes 6488064 | tf_op jit(solution)/shard_map/all_gather | solution.py:63
  35.6 292.3 %reduce-scatter.5.cloned.1.call-start = ((), (), s32[]{:S(2)}) async-start(), calls=%async_computation.10 | async-start | bytes 12976128 | tf_op jit(solution)/shard_map/reduce_scatter | solution.py:93
  84.6 19.5 %copy-start.5 = (bf16[1,3072,256]{2,1,0:T(8,128)(2,1)S(1)}, bf16[1,3072,256]{2,1,0:T(8,128)(2,1)}, u32[]{:S(2)}) copy-start(bf16[1,3072,256]{2,1,0:T(8,128)(2,1)} %param.11) | copy-start | bytes 4718596
  109.7 64.7 %copy-start.3 = (bf16[1,256,3072]{2,1,0:T(8,128)(2,1)S(1)}, bf16[1,256,3072]{2,1,0:T(8,128)(2,1)}, u32[]{:S(2)}) copy-start(bf16[1,256,3072]{2,1,0:T(8,128)(2,1)} %param.13) | copy-start | bytes 4718596
  174.4 4.7 copy-start.6
  179.1 5.1 %copy-start.4 = (bf16[1,256,3072]{2,1,0:T(8,128)(2,1)S(1)}, bf16[1,256,3072]{2,1,0:T(8,128)(2,1)}, u32[]{:S(2)}) copy-start(bf16[1,256,3072]{2,1,0:T(8,128)(2,1)} %param.13) | copy-start | bytes 4718596
  190.5 273.6 %reduce-scatter.3.cloned.1.call-start = ((), (), s32[]{:S(2)}) async-start(), calls=%async_computation.9 | async-start | bytes 12976128 | tf_op jit(solution)/shard_map/reduce_scatter | solution.py:92
  200.4 0.9 copy-start.2
  329.7 136.2 %all-to-all-start.4 = ((f32[8,1,4]{2,1,0:T(1,128)}), f32[8,1,4]{2,1,0:T(1,128)S(1)}, u32[]{:S(2)}, u32[]{:S(2)}) async-start(f32[8,1,4]{2,1,0:T(1,128)} %bitcast.5), calls=%async_computation.6 | async-start | bytes 8192 | tf_op jit(solution)/shard_map/all_to_all | solution.py:106
  465.9 15.8 %all-to-all-start.3 = ((f32[8,4,3072]{2,1,0:T(4,128)}), f32[8,4,3072]{2,1,0:T(4,128)S(1)}, u32[]{:S(2)}, u32[]{:S(2)}) async-start(f32[8,4,3072]{2,1,0:T(4,128)} %reshape.119), calls=%async_computation.4 | async-start | bytes 786432 | tf_op jit(solution)/shard_map/all_to_all | solution.py:99
  473.6 9.2 %copy-start.1 = (bf16[1,3072,256]{2,1,0:T(8,128)(2,1)S(1)}, bf16[1,3072,256]{2,1,0:T(8,128)(2,1)}, u32[]{:S(2)}) copy-start(bf16[1,3072,256]{2,1,0:T(8,128)(2,1)} %param.12) | copy-start | bytes 4718596
Sparse Core Ops, SparseCore 0:
  22.8 70.6 all-gather.5
  95.3 68.3 all-gather.3
  190.6 137.2 reduce-scatter.4
  330.3 133.7 reduce-scatter.2
where the time goes:
time: 491 us; the launch traced here: 489 us
  waiting for transfers between devices  304 us (62%)
  blocking collectives  71.7 us (15%)
  matrix products  51.9 us (11%)
  local copies, waits for them, and re-layouts  29.5 us (6%)
  starting transfers between devices  15.6 us (3%)
  between operations  13.9 us (3%)
    reduce_scatter x1, waiting for transfers between devices, local(): lax.psum_scatter(input_part, 'section', scatter_dimension=0, tiled=True)  127 us
    reduce_scatter x1, waiting for transfers between devices, local(): lax.psum_scatter(output_part, 'section', scatter_dimension=0, tiled=True)  115 us
    all_gather x1, waiting for transfers between devices, local(): lax.all_gather(recv_dy, 'section', axis=0, tiled=True)  54 us
    all_gather x1, blocking collectives, local(): lax.all_gather(recv_weight, 'section', axis=0, tiled=True)  37.2 us
    dot_general x5, matrix products, contract_first(): lax.dot_general(left, right, (((0,), (0,)), ((), ())), preferred_element_...  18.7 us
    dot_general x3, matrix products, contract_last(): lax.dot_general(left, right, (((1,), (1,)), ((), ())), preferred_element_...  14.3 us
    all_to_all x1, blocking collectives, local(): lax.all_to_all(send_x, 'expert', split_axis=0, concat_axis=0, tiled=True)  12.8 us
    all_to_all x1, blocking collectives, local(): lax.all_to_all(send_dy, 'expert', split_axis=0, concat_axis=0, tiled=True)  11.5 us
  transfers between devices with their start and end apart: 6, of which 4 were waited for; matrix products, arithmetic and copies ran while one was open for 11% of the time, Pallas kernels for 0%

commit v1 on v0

v1 whole, which is shorter than its diff:
```python
import jax
import jax.numpy as jnp
from jax import lax
from jax.sharding import PartitionSpec as P


def slot_matrix(route_ids, experts, capacity):
    flattened = route_ids.reshape(-1)
    onehot = (flattened[:, None] == jnp.arange(experts, dtype=jnp.int32)[None, :]).astype(jnp.int32)
    before = jnp.cumsum(onehot, axis=0) - onehot
    position = jnp.sum(before * onehot, axis=1)
    target = flattened * capacity + position
    columns = jnp.arange(experts * capacity, dtype=jnp.int32)
    return target[:, None] == columns[None, :]


def contract_last(left, right):
    return lax.dot_general(
        left, right, (((1,), (1,)), ((), ())), preferred_element_type=jnp.float32
    )


def contract_first(left, right):
    return lax.dot_general(
        left, right, (((0,), (0,)), ((), ())), preferred_element_type=jnp.float32
    )


def local(tokens, upstream, route_ids, route_gates, w_gate, w_up, w_down):
    experts = lax.axis_size("expert")
    tok_count, features = tokens.shape
    capacity = min(tok_count, max(2, 4 * tok_count // experts))
    chosen_slots = slot_matrix(route_ids, experts, capacity)
    placement = chosen_slots.astype(jnp.bfloat16)
    gates = route_gates.reshape(-1).astype(jnp.float32)
    tokens_twice = jnp.repeat(tokens, 2, axis=0)
    scaled = (gates[:, None] * jnp.repeat(upstream, 2, axis=0).astype(jnp.float32)).astype(
        jnp.bfloat16
    )
    send_x = contract_first(placement, tokens_twice).astype(jnp.bfloat16)
    send_u = contract_first(placement, scaled).astype(jnp.bfloat16)
    send = jnp.concatenate(
        [send_x.reshape(experts, capacity, features), send_u.reshape(experts, capacity, features)],
        axis=1,
    )
    recv = lax.all_to_all(send, "expert", split_axis=0, concat_axis=0, tiled=True)
    mine = jnp.stack([recv[:, :capacity], recv[:, capacity:]]).reshape(
        2, experts * capacity, features
    )
    every = lax.all_gather(mine, "section", axis=1, tiled=True)
    rows_x, rows_u = every[0], every[1]
    gate_slab = w_gate[0]
    up_slab = w_up[0]
    down_slab = w_down[0]
    pre_gate = jnp.dot(rows_x, gate_slab, preferred_element_type=jnp.float32)
    pre_up = jnp.dot(rows_x, up_slab, preferred_element_type=jnp.float32)
    sigmoid_gate = jax.nn.sigmoid(pre_gate)
    active = pre_gate * sigmoid_gate
    hidden = (active * pre_up).astype(jnp.bfloat16)
    d_hidden = contract_last(rows_u, down_slab)
    d_gate = (d_hidden * pre_up * (sigmoid_gate * (1.0 + pre_gate * (1.0 - sigmoid_gate)))).astype(
        jnp.bfloat16
    )
    d_up = (d_hidden * active).astype(jnp.bfloat16)
    grad_down = contract_first(hidden, rows_u)
    grad_gate = contract_first(rows_x, d_gate)
    grad_up = contract_first(rows_x, d_up)
    input_part = contract_last(d_gate, gate_slab) + contract_last(d_up, up_slab)
    gate_part = hidden.astype(jnp.float32) * d_hidden
    units = gate_part.shape[1]
    gate_part = sum(gate_part[:, i : i + 128] for i in range(0, units, 128))
    part = jnp.concatenate([input_part, gate_part], axis=1)
    part_mine = lax.psum_scatter(part, "section", scatter_dimension=0, tiled=True)
    back = lax.all_to_all(
        part_mine.reshape(experts, capacity, features + 128),
        "expert",
        split_axis=0,
        concat_axis=0,
        tiled=True,
    ).reshape(experts * capacity, features + 128)
    selector = chosen_slots.astype(jnp.float32)
    choice = jnp.dot(selector, back, precision=lax.Precision.HIGHEST)
    grad_tokens = jnp.sum(choice[:, :features].reshape(tok_count, 2, features), axis=1)
    grad_gates = (jnp.sum(choice[:, features:], axis=1) / gates).reshape(tok_count, 2)
    return (
        grad_tokens.astype(jnp.bfloat16),
        grad_gates,
        grad_gate.astype(jnp.bfloat16)[None],
        grad_up.astype(jnp.bfloat16)[None],
        grad_down.astype(jnp.bfloat16)[None],
    )


def solution(mesh):
    placed = (
        P(("section", "expert"), None),
        P(("section", "expert"), None),
        P(("section", "expert"), None),
        P(("section", "expert"), None),
        P("expert", None, "section"),
        P("expert", None, "section"),
        P("expert", "section", None),
    )
    return jax.shard_map(
        local,
        mesh=mesh,
        in_specs=placed,
        out_specs=(
            P(("section", "expert"), None),
            P(("section", "expert"), None),
            P("expert", None, "section"),
            P("expert", None, "section"),
            P("expert", "section", None),
        ),
        check_vma=False,
    )
```

time: 491 us -> 305 us (0.62)
  waiting for transfers between devices: 304 us -> 207 us
  blocking collectives: 71.7 us -> 14.6 us
  local copies, waits for them, and re-layouts: 29.5 us -> 9.77 us
  matrix products: 51.9 us -> 38 us
  other arithmetic: 2.48 us -> 12.6 us
  starting transfers between devices: 15.6 us -> 7.33 us
    reduce_scatter x2 -> x1, waiting for transfers between devices: 241 us -> 126 us  [local(): lax.psum_scatter(part, 'section', scatter_dimension=0, tiled=True)]
    all_gather x1 -> x0, blocking collectives: 37.2 us -> none  [local(): lax.all_gather(recv_weight, 'section', axis=0, tiled=True)]
    reshape x9 -> x6, local copies, waits for them, and re-layouts: 23.7 us -> 2.37 us  [the longest x1 1.87 us: local(): part_mine.reshape(experts, capacity, features + 128)]
    all_to_all x3 -> x1, blocking collectives: 34.5 us -> 14.6 us  [local(): lax.all_to_all(send, 'expert', split_axis=0, concat_axis=0, tiled=True)]
    all_gather x2 -> x1, waiting for transfers between devices: 62.8 us -> 81 us  [local(): every = lax.all_gather(mine, 'section', axis=1, tiled=True)]
    concatenate x0 -> x2, other arithmetic: none -> 10.5 us  [the longest x1 10.3 us: local(): part = jnp.concatenate([input_part, gate_part], axis=1)]
    all_to_all x2 -> x1, starting transfers between devices: 15.3 us -> 7.25 us  [local(): lax.all_to_all(part_mine.reshape(experts, capacity, features + 128), 'exp...]
    dot_general x4 -> x1, matrix products: 8.23 us -> 0.28 us  [local(): choice = jnp.dot(selector, back, precision=lax.Precision.HIGHEST)]
  transfers between devices with their start and end apart: 6 -> 3, of which waited for: 4 -> 3; matrix products, arithmetic and copies ran while one was open for 11% -> 6% of each run, Pallas kernels for 0% -> 0%
where the time goes in v1:
time: 305 us; the launch traced here: 304 us
  waiting for transfers between devices  207 us (68%)
  matrix products  38 us (12%)
  blocking collectives  14.6 us (5%)
  between operations  14.2 us (5%)
  other arithmetic  12.6 us (4%)
  local copies, waits for them, and re-layouts  9.77 us (3%)
  starting transfers between devices  7.33 us (2%)
    reduce_scatter x1, waiting for transfers between devices, local(): lax.psum_scatter(part, 'section', scatter_dimension=0, tiled=True)  126 us
    all_gather x1, waiting for transfers between devices, local(): every = lax.all_gather(mine, 'section', axis=1, tiled=True)  81 us
    dot_general x5, matrix products, contract_first(): lax.dot_general(left, right, (((0,), (0,)), ((), ())), preferred_element_...  18.4 us
    all_to_all x1, blocking collectives, local(): lax.all_to_all(send, 'expert', split_axis=0, concat_axis=0, tiled=True)  14.6 us
    dot_general x3, matrix products, contract_last(): lax.dot_general(left, right, (((1,), (1,)), ((), ())), preferred_element_...  12.7 us
    concatenate x1, other arithmetic, local(): part = jnp.concatenate([input_part, gate_part], axis=1)  10.3 us
    all_to_all x1, starting transfers between devices, local(): lax.all_to_all(part_mine.reshape(experts, capacity, features + 128), 'exp...  7.25 us
  transfers between devices with their start and end apart: 3, of which 3 were waited for; matrix products, arithmetic and copies ran while one was open for 6% of the time, Pallas kernels for 0%

profile of v1, /device:TPU:4, one launch (start us, length us, event | category | flops | bytes accessed | tf_op | source)
XLA Modules:
  0.0 304.0 jit_solution(16035402707329511470)
XLA Ops:
  7.2 0.0 copy-start
  7.2 0.0 all-gather.2.cloned.1.call-start
  7.2 0.9 copy.17
  8.1 0.1 reshape.64
  8.2 0.8 copy.16
  8.9 0.1 reshape.57
  9.0 0.1 fusion.21
  9.1 0.2 select_reduce_fusion
  9.3 0.9 broadcast_in_dim.19
  10.2 0.3 convolution_convert_fusion.1
  10.5 0.1 reshape.59
  10.6 0.9 broadcast_in_dim.20
  11.5 0.1 convert_element_type.63
  11.6 0.3 convolution_convert_fusion
  12.0 0.1 reshape.60
  12.0 0.2 pad_maximum_fusion.1
  12.2 14.6 %all_to_all.10 = bf16[8,8,3072]{2,1,0:T(8,128)(2,1)S(1)} all-to-all(bf16[8,8,3072]{2,1,0:T(8,128)(2,1)S(1)} %pad_maximum_fusion.1), channel_id=1, replica_groups=mesh['section'=32,'expert'=8] {'expert'}, dimensions={0} | all-to-all | bytes 786432 | tf_op jit(solution)/shard_map/all_to_all | solution.py:46
  26.8 0.1 fusion.25
  27.1 0.8 pad_maximum_fusion.2
  27.8 0.0 all-gather.2.cloned.1.call-update
  27.9 0.0 copy-start.2
  27.9 0.0 reduce-scatter.2.cloned.1.call-start
  27.9 81.0 %all-gather.2.cloned.1.call-done = bf16[2,1024,3072]{2,1,0:T(8,128)(2,1)} async-done(((bf16[2,32,3072]{2,1,0:T(8,128)(2,1)}), bf16[2,1024,3072]{2,1,0:T(8,128)(2,1)}) %all-gather.2.cloned.1.call-update) | async-done | bytes 12582928 | tf_op jit(solution)/shard_map/all_gather | solution.py:50
  108.9 0.0 copy-done
  108.9 0.0 copy-start.5
  108.9 4.8 %fusion.4 = f32[1024,256]{0,1:T(8,128)S(1)} fusion(bf16[2,1024,3072]{2,1,0:T(8,128)(2,1)} %all-gather.2.cloned.1.call-done, bf16[1,3072,256]{2,1,0:T(8,128)(2,1)S(1)} %copy-done), kind=kOutput, calls=%fused_computation.8 | convolution fusion | flops 1610612736 | bytes 8912896 | tf_op jit(solution)/shard_map/dot_general | solution.py:55
  113.6 0.0 copy-done.2
  113.7 1.6 copy-done.5
  115.3 0.0 copy-start.6
  115.3 1.9 fusion.5
  117.1 0.0 copy-done.6
  117.1 3.2 %convert_multiply_fusion = (f32[1024,256]{0,1:T(8,128)S(1)}, bf16[1024,256]{0,1:T(8,128)(2,1)}, bf16[1024,256]{0,1:T(8,128)(2,1)}, bf16[1024,256]{0,1:T(8,128)(2,1)S(1)}) fusion(f32[1024,256]{0,1:T(8,128)S(1)} %fusion.5, f32[1024,256]{0,1:T(8,128)S(1)} %fusion.4, bf16[1,256,3072]{2,1,0:T(8,128)(2,1)S(1)} %copy-done.6, bf16[2,1024,3072]{2,1,0:T(8,128)(2,1)S(1)} %copy-done.5), kind=kOutput, calls=%fused_computation.24 | convolution fusion | flops 1615069184 | bytes 12582912 | tf_op jit(solution)/shard_map/dot_general | solution.py:18
  120.3 0.1 slice_add_fusion
  120.4 0.2 copy.18
  120.6 0.0 copy-start.3
  120.6 3.0 fusion.12
  123.6 0.0 copy-done.3
  123.6 6.5 %convolution_add_fusion = f32[1024,3072]{1,0:T(8,128)} fusion(f32[1024,3072]{1,0:T(8,128)S(1)} %fusion.12, bf16[1024,256]{0,1:T(8,128)(2,1)S(1)} %get-tuple-element.18, bf16[1,3072,256]{2,1,0:T(8,128)(2,1)S(1)} %copy-done.3), kind=kOutput, calls=%fused_computation.1 | convolution fusion | flops 1613758464 | bytes 27262976 | tf_op jit(solution)/shard_map/dot_general | solution.py:18
  130.1 10.3 %pad_maximum_fusion = f32[1024,3200]{1,0:T(8,128)} fusion(f32[1024,128]{1,0:T(8,128)S(1)} %copy.18, f32[1024,3072]{1,0:T(8,128)} %convolution_add_fusion), kind=kLoop, calls=%fused_computation | loop fusion | flops 3276800 | bytes 26214400 | tf_op jit(solution)/shard_map/concatenate | solution.py:72
  140.4 0.0 copy-start.4
  140.4 0.0 reduce-scatter.2.cloned.1.call-update
  140.4 1.0 copy-done.4
  141.5 6.0 %fusion.11 = bf16[1,3072,256]{2,1,0:T(8,128)(2,1)} fusion(bf16[1024,256]{0,1:T(8,128)(2,1)S(1)} %copy-done.4, bf16[2,1024,3072]{2,1,0:T(8,128)(2,1)} %all-gather.2.cloned.1.call-done), kind=kOutput, calls=%fused_computation.15 | convolution fusion | flops 1611399168 | bytes 8388608 | tf_op jit(solution)/shard_map/dot_general | solution.py:24
  147.5 0.0 copy-start.7
  147.5 5.9 %fusion.10 = bf16[1,3072,256]{2,1,0:T(8,128)(2,1)} fusion(bf16[1024,256]{0,1:T(8,128)(2,1)S(1)} %get-tuple-element.18, bf16[2,1024,3072]{2,1,0:T(8,128)(2,1)} %all-gather.2.cloned.1.call-done), kind=kOutput, calls=%fused_computation.14 | convolution fusion | flops 1611399168 | bytes 8388608 | tf_op jit(solution)/shard_map/dot_general | solution.py:24
  153.4 125.7 %reduce-scatter.2.cloned.1.call-done = f32[32,3200]{1,0:T(8,128)} async-done(((f32[1024,3200]{1,0:T(8,128)}), f32[32,3200]{1,0:T(8,128)}) %reduce-scatter.2.cloned.1.call-update) | async-done | bytes 409616 | tf_op jit(solution)/shard_map/reduce_scatter | solution.py:73
  279.1 1.9 reshape.61
  281.0 7.3 %all-to-all-start.1 = ((f32[8,4,3200]{2,1,0:T(4,128)}), f32[8,4,3200]{2,1,0:T(4,128)S(1)}, u32[]{:S(2)}, u32[]{:S(2)}) async-start(f32[8,4,3200]{2,1,0:T(4,128)} %reshape.61), calls=%async_computation.2 | async-start | bytes 819200 | tf_op jit(solution)/shard_map/all_to_all | solution.py:74
  288.2 0.0 copy-start.1
  288.2 0.0 copy-done.7
  288.3 5.9 %fusion.9 = bf16[1,256,3072]{2,1,0:T(8,128)(2,1)} fusion(bf16[1024,256]{0,1:T(8,128)(2,1)S(1)} %copy-done.7, bf16[2,1024,3072]{2,1,0:T(8,128)(2,1)} %all-gather.2.cloned.1.call-done), kind=kOutput, calls=%fused_computation.13 | convolution fusion | flops 1611399168 | bytes 8388608 | tf_op jit(solution)/shard_map/dot_general | solution.py:24
  294.1 0.7 all-to-all-done.1
  294.9 0.1 reshape.62
  295.0 0.3 fusion.20
  295.3 0.1 slice_reduce_fusion
  295.4 0.1 reshape.63
  295.5 0.1 reduce_sum.32
  295.6 0.6 copy.19
  296.3 0.9 reduce_sum.30
  297.1 0.0 copy-done.1
  (7 shorter events, 0.2 us)
Async XLA Ops:
  7.2 101.7 %copy-start = (bf16[1,3072,256]{2,1,0:T(8,128)(2,1)S(1)}, bf16[1,3072,256]{2,1,0:T(8,128)(2,1)}, u32[]{:S(2)}) copy-start(bf16[1,3072,256]{2,1,0:T(8,128)(2,1)} %param.11) | copy-start | bytes 4718596
  7.2 101.7 %all-gather.2.cloned.1.call-start = ((), (), s32[]{:S(2)}) async-start(), calls=%async_computation.3 | async-start | bytes 12976128 | tf_op jit(solution)/shard_map/all_gather | solution.py:50
  27.9 85.8 %copy-start.2 = (bf16[1,3072,256]{2,1,0:T(8,128)(2,1)S(1)}, bf16[1,3072,256]{2,1,0:T(8,128)(2,1)}, u32[]{:S(2)}) copy-start(bf16[1,3072,256]{2,1,0:T(8,128)(2,1)} %param.12) | copy-start | bytes 4718596
  27.9 251.3 %reduce-scatter.2.cloned.1.call-start = ((), (), s32[]{:S(2)}) async-start(), calls=%async_computation.4 | async-start | bytes 13516800 | tf_op jit(solution)/shard_map/reduce_scatter | solution.py:73
  108.9 6.4 %copy-start.5 = (bf16[2,1024,3072]{2,1,0:T(8,128)(2,1)S(1)}, bf16[2,1024,3072]{2,1,0:T(8,128)(2,1)}, u32[]{:S(2)}) copy-start(bf16[2,1024,3072]{2,1,0:T(8,128)(2,1)} %all-gather.2.cloned.1.call-done) | copy-start | bytes 37748740
  115.3 1.9 copy-start.6
  120.6 3.0 copy-start.3
  140.4 1.0 copy-start.4
  147.5 140.8 %copy-start.7 = (bf16[1024,256]{0,1:T(8,128)(2,1)S(1)}, bf16[1024,256]{0,1:T(8,128)(2,1)}, u32[]{:S(2)}) copy-start(bf16[1024,256]{0,1:T(8,128)(2,1)} %get-tuple-element.16) | copy-start | bytes 1572868
  281.0 13.9 %all-to-all-start.1 = ((f32[8,4,3200]{2,1,0:T(4,128)}), f32[8,4,3200]{2,1,0:T(4,128)S(1)}, u32[]{:S(2)}, u32[]{:S(2)}) async-start(f32[8,4,3200]{2,1,0:T(4,128)} %reshape.61), calls=%async_computation.2 | async-start | bytes 819200 | tf_op jit(solution)/shard_map/all_to_all | solution.py:74
  288.2 8.9 %copy-start.1 = (bf16[1,3072,256]{2,1,0:T(8,128)(2,1)S(1)}, bf16[1,3072,256]{2,1,0:T(8,128)(2,1)}, u32[]{:S(2)}) copy-start(bf16[1,3072,256]{2,1,0:T(8,128)(2,1)} %param.11) | copy-start | bytes 4718596
Sparse Core Ops, SparseCore 0:
  28.0 80.8 all-gather.1
  140.6 138.5 reduce-scatter.1
